TPU v7x, 32 devices: a whole 2x2x4 slice. The times are simulated.
32 devices in a mesh: parts: 2 (over x), gy: 16 (over z, y, core).
Axes of the slice: x: 2, y: 2, z: 4, core: 2. Of those that a mesh axis runs over, the one named last changes fastest.
Arguments:
- zero_filled: float32 [32, 2, 64, 128], P(('parts', 'gy')), parts along dimension 0, may hold values from -6 to 6
- coil_maps: bfloat16 [32, 2, 32, 64, 128], P(('parts', 'gy')), parts along dimension 0, may hold values from -0.75 to 0.75
- offsets: int32 [128], P('parts'), parts along dimension 0, may hold values from 0 to 3
- step_sizes: float32 [1], replicated, may hold values from 0.6 to 1.4
- w_in: bfloat16 [64, 2, 3, 3], replicated, may hold values from -1.5 to 1.5
- b_in: float32 [64], replicated, may hold values from -0.5 to 0.5
- w_mid: bfloat16 [64, 64, 3, 3], replicated, may hold values from -0.25 to 0.25
- b_mid: float32 [64], replicated, may hold values from -0.5 to 0.5
- w_out: bfloat16 [2, 64, 3, 3], replicated, may hold values from -0.125 to 0.125
- b_out: float32 [2], replicated, may hold values from -0.5 to 0.5
Outputs:
- recon: float32 [32, 2, 64, 128], P(('parts', 'gy')), parts along dimension 0
There are 2 independent parts, one for each index of `parts`. A program takes and returns all parts, laid end to end along the dimension named above; an argument that names none is the same for every part. Nothing has to cross between parts.
Inputs may be any that keep to these rules, and one draw needn't show every extreme that they name: Readout row x samples the phase-encode lines offsets[x] + 4 m.
All inputs are finite; a program needn't handle non-finite values.
Results may differ from a plain program's by a relative error of at most 0.0012.
Values may be sent and summed in bfloat16 or wider, within the bound.
No kernel may reach another device: no remote copies, remote signals or barrier semaphores. Data moves between devices by JAX's collectives and lax.ppermute only.
A program may use at most 64 MiB of HBM per device.

v0:
```python
import jax
import jax.numpy as jnp
from jax import lax
from jax.sharding import PartitionSpec as P


def phase_tables(offsets):
    turns = jnp.arange(4, dtype=jnp.int32)[:, None] * offsets[None, :] % 4
    cosines = (turns == 0).astype(jnp.float32) - (turns == 2).astype(jnp.float32)
    sines = (turns == 3).astype(jnp.float32) - (turns == 1).astype(jnp.float32)
    return (cosines, sines)


def fold_normal(maps_list, field_list, cosines, sines):
    folded_real = None
    folded_imag = None
    for partner in range(4):
        maps_real = maps_list[partner][:, 0].astype(jnp.float32)
        maps_imag = maps_list[partner][:, 1].astype(jnp.float32)
        field_real = field_list[partner][:, 0][:, None]
        field_imag = field_list[partner][:, 1][:, None]
        coil_real = maps_real * field_real - maps_imag * field_imag
        coil_imag = maps_real * field_imag + maps_imag * field_real
        cosine = cosines[partner][None, None, :, None]
        sine = sines[partner][None, None, :, None]
        term_real = cosine * coil_real - sine * coil_imag
        term_imag = cosine * coil_imag + sine * coil_real
        if partner == 0:
            folded_real, folded_imag = (term_real, term_imag)
        else:
            folded_real = folded_real + term_real
            folded_imag = folded_imag + term_imag
    folded_real = 0.25 * folded_real
    folded_imag = 0.25 * folded_imag
    own_real = maps_list[0][:, 0].astype(jnp.float32)
    own_imag = maps_list[0][:, 1].astype(jnp.float32)
    normal_real = jnp.sum(own_real * folded_real + own_imag * folded_imag, axis=1)
    normal_imag = jnp.sum(own_real * folded_imag - own_imag * folded_real, axis=1)
    return jnp.stack([normal_real, normal_imag], axis=1)


def convolve(inputs, kernel):
    return lax.conv_general_dilated(
        inputs,
        kernel,
        (1, 1),
        "SAME",
        dimension_numbers=("NCHW", "OIHW", "NCHW"),
        preferred_element_type=jnp.float32,
    )


def denoise(stepped, w_in, b_in, w_mid, b_mid, w_out, b_out):
    stepped_low = stepped.astype(jnp.bfloat16)
    hidden_one = jax.nn.relu(convolve(stepped_low, w_in) + b_in[None, :, None, None]).astype(
        jnp.bfloat16
    )
    hidden_two = jax.nn.relu(convolve(hidden_one, w_mid) + b_mid[None, :, None, None]).astype(
        jnp.bfloat16
    )
    return stepped + convolve(hidden_two, w_out) + b_out[None, :, None, None]


def per_device(zero_filled, coil_maps, offsets, step_sizes, w_in, b_in, w_mid, b_mid, w_out, b_out):
    cosines, sines = phase_tables(offsets)
    devices = lax.axis_size("gy")
    field = zero_filled
    width_piece = zero_filled.shape[2] // devices
    first_row = lax.axis_index("gy") * width_piece
    cos_piece = lax.dynamic_slice_in_dim(cosines, first_row, width_piece, 1)
    sin_piece = lax.dynamic_slice_in_dim(sines, first_row, width_piece, 1)
    maps_whole = lax.all_to_all(coil_maps, "gy", split_axis=3, concat_axis=0, tiled=True)
    quarter = maps_whole.shape[0] // 4
    maps_list = [jnp.roll(maps_whole, -partner * quarter, axis=0) for partner in range(4)]
    whole = lax.all_to_all(field, "gy", split_axis=2, concat_axis=0, tiled=True)
    field_list = [jnp.roll(whole, -partner * quarter, axis=0) for partner in range(4)]
    normal_whole = fold_normal(maps_list, field_list, cos_piece, sin_piece)
    normal = lax.all_to_all(normal_whole, "gy", split_axis=0, concat_axis=2, tiled=True)
    stepped = field - step_sizes[0] * (normal - zero_filled)
    field = denoise(stepped, w_in, b_in, w_mid, b_mid, w_out, b_out)
    return field


def solution(mesh):
    in_specs = (
        P(("parts", "gy"), None, None, None),
        P(("parts", "gy"), None, None, None, None),
        P("parts"),
        P(),
        P(),
        P(),
        P(),
        P(),
        P(),
        P(),
    )
    out_specs = P(("parts", "gy"), None, None, None)
    return jax.shard_map(
        per_device, mesh=mesh, in_specs=in_specs, out_specs=out_specs, check_vma=False
    )
```

profile of v0, /device:TPU:0, one launch (start us, length us, event | category | flops | bytes accessed | tf_op | source)
XLA Modules:
  0.0 121.8 jit_solution(7083519290412785793)
XLA Ops:
  0.0 1.6 %copy.53 = f32[1,2,64,128]{3,1,0,2:T(2,128)} copy(f32[1,2,64,128]{3,2,1,0:T(8,128)} %param.10) | data formatting | bytes 131072 | tf_op args[0]
  1.6 7.4 %all-to-all-start.1 = ((f32[1,2,64,128]{3,1,0,2:T(2,128)}), f32[1,2,64,128]{3,1,0,2:T(2,128)S(1)}, u32[]{:S(2)}, u32[]{:S(2)}) async-start(f32[1,2,64,128]{3,1,0,2:T(2,128)} %copy.53), calls=%async_computation.1 | async-start | bytes 131072 | tf_op jit(solution)/shard_map/all_to_all | solution.py:75
  9.0 2.9 %copy.49 = bf16[1,2,32,64,128]{4,2,1,0,3:T(8,128)(2,1)} copy(bf16[1,2,32,64,128]{4,3,2,1,0:T(8,128)(2,1)} %param.11) | data formatting | bytes 2097152 | tf_op args[1]
  11.9 4.0 %all-to-all-done.1 = f32[1,2,64,128]{3,1,0,2:T(2,128)S(1)} async-done(((f32[1,2,64,128]{3,1,0,2:T(2,128)}), f32[1,2,64,128]{3,1,0,2:T(2,128)S(1)}, u32[]{:S(2)}, u32[]{:S(2)}) %all-to-all-start.1) | async-done | bytes 65568 | tf_op jit(solution)/shard_map/all_to_all | solution.py:75
  15.9 3.7 %all-to-all-start = ((bf16[1,2,32,64,128]{4,2,1,0,3:T(8,128)(2,1)}), bf16[1,2,32,64,128]{4,2,1,0,3:T(8,128)(2,1)S(1)}, u32[]{:S(2)}, u32[]{:S(2)}) async-start(bf16[1,2,32,64,128]{4,2,1,0,3:T(8,128)(2,1)} %copy.49), calls=%async_computation | async-start | bytes 2097152 | tf_op jit(solution)/shard_map/all_to_all | solution.py:72
  19.6 0.1 constant_dynamic-slice_fusion
  19.8 22.6 %all-to-all-done = bf16[1,2,32,64,128]{4,2,1,0,3:T(8,128)(2,1)S(1)} async-done(((bf16[1,2,32,64,128]{4,2,1,0,3:T(8,128)(2,1)}), bf16[1,2,32,64,128]{4,2,1,0,3:T(8,128)(2,1)S(1)}, u32[]{:S(2)}, u32[]{:S(2)}) %all-to-all-start) | async-done | bytes 1048608 | tf_op jit(solution)/shard_map/all_to_all | solution.py:72
  42.4 0.1 copy.50
  42.5 0.4 slice_bitcast_fusion
  42.9 0.1 slice_bitcast_fusion.3
  43.0 0.1 copy.69
  43.1 0.0 copy-start.1
  43.1 0.0 copy-start.4
  43.1 0.0 copy-start.6
  43.1 0.0 copy-start.8
  43.1 2.8 %fusion.37 = (f32[16,4,128]{2,1,0:T(4,128)S(1)}, f32[16,4,128]{2,1,0:T(4,128)S(1)}) fusion(bf16[16,2,32,4,128]{4,2,1,3,0:T(8,128)(2,1)S(1)} %bitcast.193, bf16[16,2,32,4,128]{4,2,3,1,0:T(8,128)(2,1)S(1)} %bitcast.194, f32[4]{0:T(128)S(1)} %get-tuple-element.38, f32[16,4,128]{2,1,0:T(4,128)S(1)} %get-tuple-element.32, ...), kind=kLoop, calls=%fused_computation.57 | loop fusion | flops 25149440 | bytes 4522112 | tf_op jit(solution)/shard_map/reduce_sum | solution.py:37
  45.9 0.6 pad_maximum_fusion.3
  46.5 6.8 %all-to-all-start.2 = ((f32[16,2,4,128]{3,2,1,0:T(4,128)}), f32[16,2,4,128]{3,2,1,0:T(4,128)S(1)}, u32[]{:S(2)}, u32[]{:S(2)}) async-start(f32[16,2,4,128]{3,2,1,0:T(4,128)} %pad_maximum_fusion.3), calls=%async_computation.2 | async-start | bytes 131072 | tf_op jit(solution)/shard_map/all_to_all | solution.py:78
  54.0 6.2 %all-to-all-done.2 = f32[16,2,4,128]{3,2,1,0:T(4,128)S(1)} async-done(((f32[16,2,4,128]{3,2,1,0:T(4,128)}), f32[16,2,4,128]{3,2,1,0:T(4,128)S(1)}, u32[]{:S(2)}, u32[]{:S(2)}) %all-to-all-start.2) | async-done | bytes 65568 | tf_op jit(solution)/shard_map/all_to_all | solution.py:78
  60.3 0.1 copy.65
  60.4 0.1 pad.clone
  60.5 0.6 copy.58
  61.1 0.1 slice.240
  61.3 3.7 %fusion.21 = bf16[64,1,8,17,64]{4,2,3,0,1:T(8,128)(2,1)S(1)} fusion(f32[64]{0:T(128)S(1)} %copy-done.6, pred[8,17]{0,1:T(8,128)(4,1)S(1)} %copy-done.8, bf16[64,2,3,3]{0,1,3,2:T(2,128)(2,1)S(1)} %copy-done.4, bf16[2,64,1,7,2]{3,0,4,1,2:T(2,128)(2,1)S(1)} %slice.240, bf16[2,64,1,8,17]{3,0,4,1,2:T(2,128)(2,1)S(1)} %copy.58), kind=kOutput, calls=%fused_computation.23 | convolution fusion | flops 22747136 | bytes 1155208 | tf_op jit(solution)/shard_map/conv_general_dilated | solution.py:43
  65.0 0.1 fusion.76
  65.1 5.6 %fusion.23 = bf16[64,1,8,17,64]{4,2,3,0,1:T(8,128)(2,1)S(1)} fusion(f32[64]{0:T(128)S(1)} %copy-done.7, pred[8,17]{0,1:T(8,128)(4,1)S(1)} %copy-done.8, bf16[64,64,3,3]{1,0,3,2:T(8,128)(2,1)S(1)} %copy-done, bf16[64,1,7,1,64]{4,2,3,0,1:T(8,128)(2,1)S(1)} %get-tuple-element.10, bf16[64,1,7,1,64]{4,2,3,0,1:T(8,128)(2,1)S(1)} %get-tuple-element.9, ...), kind=kOutput, calls=%fused_computation.25 | convolution fusion | flops 643497984 | bytes 2417032 | tf_op jit(solution)/shard_map/conv_general_dilated | solution.py:43
  70.6 0.1 fusion.75
  70.7 49.3 %fusion.18 = f32[64,8,17,2]{1,3,2,0:T(2,128)S(1)} fusion(bf16[2,64,3,3]{1,0,3,2:T(2,128)(2,1)S(1)} %copy-done.5, bf16[64,1,7,1,64]{4,2,3,0,1:T(8,128)(2,1)S(1)} %get-tuple-element.8, bf16[64,1,7,1,64]{4,2,3,0,1:T(8,128)(2,1)S(1)} %get-tuple-element.7, bf16[64,1,8,17,64]{4,2,3,0,1:T(8,128)(2,1)S(1)} %fusion.23), kind=kOutput, calls=%fused_computation.20 | convolution fusion | flops 26071040 | bytes 1300736 | tf_op jit(solution)/shard_map/conv_general_dilated | solution.py:43
  120.0 1.0 copy.59
  121.0 0.1 copy.64
  121.1 0.0 copy-done.2
  121.1 0.7 fusion.53
  (26 shorter events, 0.2 us)
Async XLA Ops:
  0.0 65.0 %copy-start = (bf16[64,64,3,3]{1,0,3,2:T(8,128)(2,1)S(1)}, bf16[64,64,3,3]{1,0,3,2:T(8,128)(2,1)}, u32[]{:S(2)}) copy-start(bf16[64,64,3,3]{1,0,3,2:T(8,128)(2,1)} %param.16) | copy-start | bytes 221188
  0.0 19.5 %copy-start.3 = (s32[64]{0:T(128)S(1)}, s32[64]{0:T(128)}, u32[]{:S(2)}) copy-start(s32[64]{0:T(128)} %param.12) | copy-start | bytes 772
  1.6 14.3 %all-to-all-start.1 = ((f32[1,2,64,128]{3,1,0,2:T(2,128)}), f32[1,2,64,128]{3,1,0,2:T(2,128)S(1)}, u32[]{:S(2)}, u32[]{:S(2)}) async-start(f32[1,2,64,128]{3,1,0,2:T(2,128)} %copy.53), calls=%async_computation.1 | async-start | bytes 131072 | tf_op jit(solution)/shard_map/all_to_all | solution.py:75
  15.9 26.6 %all-to-all-start = ((bf16[1,2,32,64,128]{4,2,1,0,3:T(8,128)(2,1)}), bf16[1,2,32,64,128]{4,2,1,0,3:T(8,128)(2,1)S(1)}, u32[]{:S(2)}, u32[]{:S(2)}) async-start(bf16[1,2,32,64,128]{4,2,1,0,3:T(8,128)(2,1)} %copy.49), calls=%async_computation | async-start | bytes 2097152 | tf_op jit(solution)/shard_map/all_to_all | solution.py:72
  43.1 17.2 %copy-start.1 = (f32[1,2,64,128]{3,2,1,0:T(8,128)S(1)}, f32[1,2,64,128]{3,2,1,0:T(8,128)}, u32[]{:S(2)}) copy-start(f32[1,2,64,128]{3,2,1,0:T(8,128)} %param.10) | copy-start | bytes 196612
  43.1 18.2 %copy-start.4 = (bf16[64,2,3,3]{0,1,3,2:T(2,128)(2,1)S(1)}, bf16[64,2,3,3]{0,1,3,2:T(2,128)(2,1)}, u32[]{:S(2)}) copy-start(bf16[64,2,3,3]{0,1,3,2:T(2,128)(2,1)} %param.14) | copy-start | bytes 6916
  43.1 18.2 %copy-start.6 = (f32[64]{0:T(128)S(1)}, f32[64]{0:T(128)}, u32[]{:S(2)}) copy-start(f32[64]{0:T(128)} %param.15) | copy-start | bytes 772
  43.1 18.2 %copy-start.8 = (pred[8,17]{0,1:T(8,128)(4,1)S(1)}, pred[8,17]{0,1:T(8,128)(4,1)}, u32[]{:S(2)}) copy-start(pred[8,17]{0,1:T(8,128)(4,1)} %constant.47) | copy-start | bytes 412
  46.5 13.7 %all-to-all-start.2 = ((f32[16,2,4,128]{3,2,1,0:T(4,128)}), f32[16,2,4,128]{3,2,1,0:T(4,128)S(1)}, u32[]{:S(2)}, u32[]{:S(2)}) async-start(f32[16,2,4,128]{3,2,1,0:T(4,128)} %pad_maximum_fusion.3), calls=%async_computation.2 | async-start | bytes 131072 | tf_op jit(solution)/shard_map/all_to_all | solution.py:78
  61.3 3.8 %copy-start.7 = (f32[64]{0:T(128)S(1)}, f32[64]{0:T(128)}, u32[]{:S(2)}) copy-start(f32[64]{0:T(128)} %param.17) | copy-start | bytes 772
  65.0 5.6 %copy-start.5 = (bf16[2,64,3,3]{1,0,3,2:T(2,128)(2,1)S(1)}, bf16[2,64,3,3]{1,0,3,2:T(2,128)(2,1)}, u32[]{:S(2)}) copy-start(bf16[2,64,3,3]{1,0,3,2:T(2,128)(2,1)} %param.18) | copy-start | bytes 6916
  70.7 50.4 %copy-start.2 = (f32[2]{0:T(128)S(1)}, f32[2]{0:T(128)}, u32[]{:S(2)}) copy-start(f32[2]{0:T(128)} %param.19) | copy-start | bytes 28
where the time goes:
time: 122 us
  matrix products  58.5 us (48%)
  waiting for transfers between devices  32.9 us (27%)
  starting transfers between devices  17.9 us (15%)
  local copies, waits for them, and re-layouts  7.39 us (6%)
  other arithmetic  4.21 us (3%)
    conv_general_dilated x3, matrix products, convolve(): lax.conv_general_dilated(inputs, kernel, (1, 1), 'SAME', dimension_number...  58.5 us
    all_to_all x1, waiting for transfers between devices, per_device(): lax.all_to_all(coil_maps, 'gy', split_axis=3, concat_axis=0, tiled=True)  22.6 us
    all_to_all x1, starting transfers between devices, per_device(): whole = lax.all_to_all(field, 'gy', split_axis=2, concat_axis=0, tiled=True)  7.39 us
    all_to_all x1, starting transfers between devices, per_device(): lax.all_to_all(normal_whole, 'gy', split_axis=0, concat_axis=2, tiled=True)  6.81 us
    all_to_all x1, waiting for transfers between devices, per_device(): lax.all_to_all(normal_whole, 'gy', split_axis=0, concat_axis=2, tiled=True)  6.25 us
    unnamed x22, local copies, waits for them, and re-layouts  4.72 us
    all_to_all x1, waiting for transfers between devices, per_device(): whole = lax.all_to_all(field, 'gy', split_axis=2, concat_axis=0, tiled=True)  4 us
    all_to_all x1, starting transfers between devices, per_device(): lax.all_to_all(coil_maps, 'gy', split_axis=3, concat_axis=0, tiled=True)  3.65 us
  transfers between devices with their start and end apart: 3, of which 3 were waited for; matrix products, arithmetic and copies ran while one was open for 3% of the time, Pallas kernels for 0%

commit v1 on v0

--- a/solution.py
+++ b/solution.py
@@ -69,7 +69,12 @@
     first_row = lax.axis_index("gy") * width_piece
     cos_piece = lax.dynamic_slice_in_dim(cosines, first_row, width_piece, 1)
     sin_piece = lax.dynamic_slice_in_dim(sines, first_row, width_piece, 1)
-    maps_whole = lax.all_to_all(coil_maps, "gy", split_axis=3, concat_axis=0, tiled=True)
+    maps_whole = jnp.concatenate(
+        jax.lax.all_to_all(
+            jnp.stack(jnp.split(coil_maps, jax.lax.axis_size("gy"), axis=3)), "gy", 0, 0
+        ),
+        axis=0,
+    )
     quarter = maps_whole.shape[0] // 4
     maps_list = [jnp.roll(maps_whole, -partner * quarter, axis=0) for partner in range(4)]
     whole = lax.all_to_all(field, "gy", split_axis=2, concat_axis=0, tiled=True)

time: 122 us -> 131 us (1.074)
  local copies, waits for them, and re-layouts: 7.39 us -> 17.4 us
  waiting for transfers between devices: 32.9 us -> 28.9 us
  starting transfers between devices: 17.9 us -> 20.3 us
    unnamed x22 -> x36, local copies, waits for them, and re-layouts: 4.72 us -> 11.4 us
    all_to_all x1, waiting for transfers between devices: 4 us -> 0.01 us  [per_device(): whole = lax.all_to_all(field, 'gy', split_axis=2, concat_axis=0, tiled=True)]
    split x0 -> x1, local copies, waits for them, and re-layouts: none -> 2.44 us  [per_device(): jnp.split(coil_maps, jax.lax.axis_size('gy'), axis=3)]
    all_to_all x1, starting transfers between devices: 3.65 us -> 6 us  [per_device(): jax.lax.all_to_all(jnp.stack(jnp.split(coil_maps, jax.lax.axis_size('gy')...]
  transfers between devices with their start and end apart: 3 -> 3, of which waited for: 3 -> 2; matrix products, arithmetic and copies ran while one was open for 3% -> 10% of each run, Pallas kernels for 0% -> 0%
where the time goes in v1:
time: 131 us; the launch traced here: 130 us
  matrix products  58.5 us (45%)
  waiting for transfers between devices  28.9 us (22%)
  starting transfers between devices  20.3 us (15%)
  local copies, waits for them, and re-layouts  17.4 us (13%)
  other arithmetic  4.2 us (3%)
    conv_general_dilated x3, matrix products, convolve(): lax.conv_general_dilated(inputs, kernel, (1, 1), 'SAME', dimension_number...  58.5 us
    all_to_all x1, waiting for transfers between devices, per_device(): jax.lax.all_to_all(jnp.stack(jnp.split(coil_maps, jax.lax.axis_size('gy')...  22.7 us
    unnamed x36, local copies, waits for them, and re-layouts  11.4 us
    all_to_all x1, starting transfers between devices, per_device(): whole = lax.all_to_all(field, 'gy', split_axis=2, concat_axis=0, tiled=True)  7.39 us
    all_to_all x1, starting transfers between devices, per_device(): lax.all_to_all(normal_whole, 'gy', split_axis=0, concat_axis=2, tiled=True)  6.86 us
    all_to_all x1, waiting for transfers between devices, per_device(): lax.all_to_all(normal_whole, 'gy', split_axis=0, concat_axis=2, tiled=True)  6.25 us
    all_to_all x1, starting transfers between devices, per_device(): jax.lax.all_to_all(jnp.stack(jnp.split(coil_maps, jax.lax.axis_size('gy')...  6 us
    reduce_sum x1, other arithmetic, fold_normal(): jnp.sum(own_real * folded_real + own_imag * folded_imag, axis=1)  2.76 us
  transfers between devices with their start and end apart: 3, of which 2 were waited for; matrix products, arithmetic and copies ran while one was open for 10% of the time, Pallas kernels for 0%

profile of v1, /device:TPU:0, one launch (start us, length us, event | category | flops | bytes accessed | tf_op | source)
XLA Modules:
  0.0 130.3 jit_solution(12793959677542863951)
XLA Ops:
  0.0 1.6 %copy.113 = f32[1,2,64,128]{3,1,0,2:T(2,128)} copy(f32[1,2,64,128]{3,2,1,0:T(8,128)} %param.10) | data formatting | bytes 131072 | tf_op args[0]
  1.6 7.4 %all-to-all-start.1 = ((f32[1,2,64,128]{3,1,0,2:T(2,128)}), f32[1,2,64,128]{3,1,0,2:T(2,128)S(1)}, u32[]{:S(2)}, u32[]{:S(2)}) async-start(f32[1,2,64,128]{3,1,0,2:T(2,128)} %copy.113), calls=%async_computation.1 | async-start | bytes 131072 | tf_op jit(solution)/shard_map/all_to_all | solution.py:80
  9.0 2.4 %fusion.96 = (bf16[1,2,32,4,128]{4,3,2,1,0:T(4,128)(2,1)S(1)}, bf16[1,2,32,4,128]{4,3,2,1,0:T(4,128)(2,1)S(1)}, bf16[1,2,32,4,128]{4,3,2,1,0:T(4,128)(2,1)S(1)},...) fusion(bf16[1,2,32,64,128]{4,3,2,1,0:T(8,128)(2,1)} %param.11), kind=kLoop, calls=%fused_computation.188 | loop fusion | bytes 2097152 | tf_op jit(solution)/shard_map/split | solution.py:74
  11.4 0.6 fusion.68
  12.0 0.6 fusion.67
  12.7 0.6 fusion.66
  13.3 0.6 fusion.65
  14.0 0.6 fusion.64
  14.6 0.6 fusion.63
  15.2 0.6 fusion.62
  15.9 0.6 fusion.61
  16.5 0.6 fusion.60
  17.2 0.6 fusion.59
  17.8 0.6 fusion.58
  18.4 0.6 fusion.57
  19.1 0.6 fusion.56
  19.7 0.6 fusion.55
  20.3 0.6 fusion.54
  21.0 0.6 fusion.53
  21.6 6.0 %all-to-all-start = ((bf16[16,1,2,32,4,128]{5,3,4,2,1,0:T(8,128)(2,1)}), bf16[16,1,2,32,4,128]{5,3,4,2,1,0:T(8,128)(2,1)S(1)}, u32[]{:S(2)}, u32[]{:S(2)}) async-start(bf16[16,1,2,32,4,128]{5,3,4,2,1,0:T(8,128)(2,1)} %fusion.53), calls=%async_computation | async-start | bytes 2097152 | tf_op jit(solution)/shard_map/all_to_all | solution.py:73
  27.9 22.7 %all-to-all-done = bf16[16,1,2,32,4,128]{5,3,4,2,1,0:T(8,128)(2,1)S(1)} async-done(((bf16[16,1,2,32,4,128]{5,3,4,2,1,0:T(8,128)(2,1)}), bf16[16,1,2,32,4,128]{5,3,4,2,1,0:T(8,128)(2,1)S(1)}, u32[]{:S(2)}, u32[]{:S(2)}) %all-to-all-start) | async-done | bytes 1048608 | tf_op jit(solution)/shard_map/all_to_all | solution.py:73
  50.6 0.4 fusion.94
  51.6 2.8 %fusion.37 = (f32[16,4,128]{2,1,0:T(4,128)S(1)}, f32[16,4,128]{2,1,0:T(4,128)S(1)}) fusion(bf16[16,2,32,4,128]{4,2,3,1,0:T(8,128)(2,1)S(1)} %bitcast.245, f32[4]{0:T(128)S(1)} %get-tuple-element.54, f32[16,4,128]{2,1,0:T(4,128)S(1)} %get-tuple-element.48, bf16[12,2,32,4,128]{4,2,3,0,1:T(8,128)(2,1)S(1)} %get-tuple-element.65, ...), kind=kLoop, calls=%fused_computation.57 | loop fusion | flops 25149440 | bytes 4522112 | tf_op jit(solution)/shard_map/reduce_sum | solution.py:37
  54.3 0.6 pad_maximum_fusion.3
  55.0 6.9 %all-to-all-start.2 = ((f32[16,2,4,128]{3,2,1,0:T(4,128)}), f32[16,2,4,128]{3,2,1,0:T(4,128)S(1)}, u32[]{:S(2)}, u32[]{:S(2)}) async-start(f32[16,2,4,128]{3,2,1,0:T(4,128)} %pad_maximum_fusion.3), calls=%async_computation.2 | async-start | bytes 131072 | tf_op jit(solution)/shard_map/all_to_all | solution.py:83
  62.5 6.2 %all-to-all-done.2 = f32[16,2,4,128]{3,2,1,0:T(4,128)S(1)} async-done(((f32[16,2,4,128]{3,2,1,0:T(4,128)}), f32[16,2,4,128]{3,2,1,0:T(4,128)S(1)}, u32[]{:S(2)}, u32[]{:S(2)}) %all-to-all-start.2) | async-done | bytes 65568 | tf_op jit(solution)/shard_map/all_to_all | solution.py:83
  69.0 0.6 copy.124
  69.8 3.7 %fusion.21 = bf16[64,1,8,17,64]{4,2,3,0,1:T(8,128)(2,1)S(1)} fusion(f32[64]{0:T(128)S(1)} %copy-done.6, pred[8,17]{0,1:T(8,128)(4,1)S(1)} %copy-done.8, bf16[64,2,3,3]{0,1,3,2:T(2,128)(2,1)S(1)} %copy-done.4, bf16[2,64,1,7,2]{3,0,4,1,2:T(2,128)(2,1)S(1)} %slice.240, bf16[2,64,1,8,17]{3,0,4,1,2:T(2,128)(2,1)S(1)} %copy.124), kind=kOutput, calls=%fused_computation.23 | convolution fusion | flops 22747136 | bytes 1155208 | tf_op jit(solution)/shard_map/conv_general_dilated | solution.py:43
  73.5 5.6 %fusion.23 = bf16[64,1,8,17,64]{4,2,3,0,1:T(8,128)(2,1)S(1)} fusion(f32[64]{0:T(128)S(1)} %copy-done.7, pred[8,17]{0,1:T(8,128)(4,1)S(1)} %copy-done.8, bf16[64,64,3,3]{1,0,3,2:T(8,128)(2,1)S(1)} %copy-done, bf16[64,1,7,1,64]{4,2,3,0,1:T(8,128)(2,1)S(1)} %get-tuple-element.10, bf16[64,1,7,1,64]{4,2,3,0,1:T(8,128)(2,1)S(1)} %get-tuple-element.9, ...), kind=kOutput, calls=%fused_computation.25 | convolution fusion | flops 643497984 | bytes 2417032 | tf_op jit(solution)/shard_map/conv_general_dilated | solution.py:43
  79.2 49.3 %fusion.18 = f32[64,8,17,2]{1,3,2,0:T(2,128)S(1)} fusion(bf16[2,64,3,3]{1,0,3,2:T(2,128)(2,1)S(1)} %copy-done.5, bf16[64,1,7,1,64]{4,2,3,0,1:T(8,128)(2,1)S(1)} %get-tuple-element.8, bf16[64,1,7,1,64]{4,2,3,0,1:T(8,128)(2,1)S(1)} %get-tuple-element.7, bf16[64,1,8,17,64]{4,2,3,0,1:T(8,128)(2,1)S(1)} %fusion.23), kind=kOutput, calls=%fused_computation.20 | convolution fusion | flops 26071040 | bytes 1300736 | tf_op jit(solution)/shard_map/conv_general_dilated | solution.py:43
  128.4 1.0 copy.125
  129.6 0.7 fusion.69
  (43 shorter events, 1.4 us)
Async XLA Ops:
  0.0 73.5 %copy-start = (bf16[64,64,3,3]{1,0,3,2:T(8,128)(2,1)S(1)}, bf16[64,64,3,3]{1,0,3,2:T(8,128)(2,1)}, u32[]{:S(2)}) copy-start(bf16[64,64,3,3]{1,0,3,2:T(8,128)(2,1)} %param.16) | copy-start | bytes 221188
  1.6 20.0 %all-to-all-start.1 = ((f32[1,2,64,128]{3,1,0,2:T(2,128)}), f32[1,2,64,128]{3,1,0,2:T(2,128)S(1)}, u32[]{:S(2)}, u32[]{:S(2)}) async-start(f32[1,2,64,128]{3,1,0,2:T(2,128)} %copy.113), calls=%async_computation.1 | async-start | bytes 131072 | tf_op jit(solution)/shard_map/all_to_all | solution.py:80
  11.4 16.2 %copy-start.3 = (s32[64]{0:T(128)S(1)}, s32[64]{0:T(128)}, u32[]{:S(2)}) copy-start(s32[64]{0:T(128)} %param.12) | copy-start | bytes 772
  21.6 29.0 %all-to-all-start = ((bf16[16,1,2,32,4,128]{5,3,4,2,1,0:T(8,128)(2,1)}), bf16[16,1,2,32,4,128]{5,3,4,2,1,0:T(8,128)(2,1)S(1)}, u32[]{:S(2)}, u32[]{:S(2)}) async-start(bf16[16,1,2,32,4,128]{5,3,4,2,1,0:T(8,128)(2,1)} %fusion.53), calls=%async_computation | async-start | bytes 2097152 | tf_op jit(solution)/shard_map/all_to_all | solution.py:73
  51.5 17.2 %copy-start.1 = (f32[1,2,64,128]{3,2,1,0:T(8,128)S(1)}, f32[1,2,64,128]{3,2,1,0:T(8,128)}, u32[]{:S(2)}) copy-start(f32[1,2,64,128]{3,2,1,0:T(8,128)} %param.10) | copy-start | bytes 196612
  51.5 18.2 %copy-start.4 = (bf16[64,2,3,3]{0,1,3,2:T(2,128)(2,1)S(1)}, bf16[64,2,3,3]{0,1,3,2:T(2,128)(2,1)}, u32[]{:S(2)}) copy-start(bf16[64,2,3,3]{0,1,3,2:T(2,128)(2,1)} %param.14) | copy-start | bytes 6916
  51.5 18.2 %copy-start.6 = (f32[64]{0:T(128)S(1)}, f32[64]{0:T(128)}, u32[]{:S(2)}) copy-start(f32[64]{0:T(128)} %param.15) | copy-start | bytes 772
  51.5 18.2 %copy-start.8 = (pred[8,17]{0,1:T(8,128)(4,1)S(1)}, pred[8,17]{0,1:T(8,128)(4,1)}, u32[]{:S(2)}) copy-start(pred[8,17]{0,1:T(8,128)(4,1)} %constant.47) | copy-start | bytes 412
  55.0 13.8 %all-to-all-start.2 = ((f32[16,2,4,128]{3,2,1,0:T(4,128)}), f32[16,2,4,128]{3,2,1,0:T(4,128)S(1)}, u32[]{:S(2)}, u32[]{:S(2)}) async-start(f32[16,2,4,128]{3,2,1,0:T(4,128)} %pad_maximum_fusion.3), calls=%async_computation.2 | async-start | bytes 131072 | tf_op jit(solution)/shard_map/all_to_all | solution.py:83
  69.8 3.8 %copy-start.7 = (f32[64]{0:T(128)S(1)}, f32[64]{0:T(128)}, u32[]{:S(2)}) copy-start(f32[64]{0:T(128)} %param.17) | copy-start | bytes 772
  73.5 5.6 %copy-start.5 = (bf16[2,64,3,3]{1,0,3,2:T(2,128)(2,1)S(1)}, bf16[2,64,3,3]{1,0,3,2:T(2,128)(2,1)}, u32[]{:S(2)}) copy-start(bf16[2,64,3,3]{1,0,3,2:T(2,128)(2,1)} %param.18) | copy-start | bytes 6916
  79.2 50.4 %copy-start.2 = (f32[2]{0:T(128)S(1)}, f32[2]{0:T(128)}, u32[]{:S(2)}) copy-start(f32[2]{0:T(128)} %param.19) | copy-start | bytes 28
